TPU v7x, 256 devices: a whole 4x4x8 slice. The times are simulated.
256 devices in a mesh: seq: 128 (over x_lo, y, z, core), head: 2 (over x_hi).
Axes of the slice: x: 4 (x_hi: 2, x_lo: 2; x = x_hi * 2 + x_lo), y: 4, z: 8, core: 2. Of those that a mesh axis runs over, the one named last changes fastest.
Arguments:
- query: bfloat16 [32768, 3584], P('seq', 'head'), may hold values from -6 to 6
- key: bfloat16 [32768, 512], P('seq', 'head'), may hold values from -6 to 6
- value: bfloat16 [32768, 512], P('seq', 'head'), may hold values from -6 to 6
- output: bfloat16 [32768, 3584], P('seq', 'head'), may hold values from -6 to 6
- output_gradient: bfloat16 [32768, 3584], P('seq', 'head'), may hold values from -6 to 6
- lse: float32 [28, 32768], P('head', 'seq'), may hold values from 3 to 6
- doc_lengths: int32 [32], replicated, may hold values from 1 to 2048, as said below
- w_query: bfloat16 [3584, 3584], P('seq', 'head'), may hold values from -0.09375 to 0.09375
- key_weight: bfloat16 [3584, 512], P('seq', 'head'), may hold values from -0.09375 to 0.09375
- value_weight: bfloat16 [3584, 512], P('seq', 'head'), may hold values from -0.09375 to 0.09375
Outputs:
- grad_input: bfloat16 [32768, 3584], P('seq', 'head')
Inputs may be any that keep to these rules, and one draw needn't show every extreme that they name: `doc_lengths`: the documents lie end to end and fill the 32768 tokens of the pack; the first has 1024 tokens, and one of exactly 2048 tokens begins at token 15360.
All inputs are finite; a program needn't handle non-finite values.
Results may differ from a plain program's by a relative error of at most 0.0056.
Values may be sent and summed in bfloat16 or wider, within the bound.
A program may use at most 128 MiB of HBM per device.

v0:
```python
import math
import jax
import jax.numpy as jnp
from jax import lax
from jax.sharding import PartitionSpec as P

HEAD_SIZE = 128
WINDOW = 512


def shifted(array, axis, by):
    peers = lax.axis_size(axis)
    pairs = [(i, i + by) for i in range(peers) if 0 <= i + by < peers]
    return lax.ppermute(array, axis, pairs)


def lower_bounds(positions, doc_lengths, window):
    starts = jnp.cumsum(doc_lengths, dtype=jnp.int32) - doc_lengths
    inside = starts[None, :] <= positions[:, None]
    doc_begin = jnp.max(jnp.where(inside, starts[None, :], 0), axis=1)
    return jnp.maximum(doc_begin, positions - window + 1)


def attend(
    query_rows,
    key_row_block,
    value_row_block,
    visible,
    logsumexp_rows,
    output_grad_rows,
    row_delta,
    score_scale,
):
    scores = (
        jnp.einsum("tgjd,kgd->gjtk", query_rows, key_row_block, preferred_element_type=jnp.float32)
        * score_scale
    )
    prob_full = jnp.where(visible[None, None], jnp.exp(scores - logsumexp_rows[..., None]), 0.0)
    prob_low = prob_full.astype(jnp.bfloat16)
    grad_val = jnp.einsum(
        "gjtk,tgjd->kgd", prob_low, output_grad_rows, preferred_element_type=jnp.float32
    )
    grad_prob = jnp.einsum(
        "tgjd,kgd->gjtk", output_grad_rows, value_row_block, preferred_element_type=jnp.float32
    )
    dscore = (prob_full * (grad_prob - row_delta[..., None]) * score_scale).astype(jnp.bfloat16)
    grad_qry = jnp.einsum(
        "gjtk,kgd->tgjd", dscore, key_row_block, preferred_element_type=jnp.float32
    )
    grad_key = jnp.einsum("gjtk,tgjd->kgd", dscore, query_rows, preferred_element_type=jnp.float32)
    return (grad_qry, grad_key, grad_val)


def projector(grad_rows, w_piece):
    return jnp.einsum("tc,rc->tr", grad_rows, w_piece, preferred_element_type=jnp.float32)


def shards(
    query, key, value, output, output_gradient, lse, doc_lengths, w_query, key_weight, value_weight
):
    tok_rows = query.shape[0]
    key_value_width = key.shape[1]
    kv_heads = key_value_width // HEAD_SIZE
    q_heads = query.shape[1] // HEAD_SIZE
    per_group = q_heads // kv_heads
    score_scale = 1.0 / math.sqrt(HEAD_SIZE)
    seq_index = lax.axis_index("seq")
    positions = seq_index * tok_rows + jnp.arange(tok_rows, dtype=jnp.int32)
    lower = lower_bounds(positions, doc_lengths, WINDOW)
    query_rows = query.reshape(tok_rows, kv_heads, per_group, HEAD_SIZE)
    output_rows = output.reshape(tok_rows, kv_heads, per_group, HEAD_SIZE)
    output_grad_rows = output_gradient.reshape(tok_rows, kv_heads, per_group, HEAD_SIZE)
    row_delta = jnp.einsum(
        "tgjd,tgjd->gjt", output_grad_rows, output_rows, preferred_element_type=jnp.float32
    )
    logsumexp_rows = lse.reshape(kv_heads, per_group, tok_rows)
    near_pair = shifted((key, value), "seq", 1)
    far_pair = shifted((key, value), "seq", 2)
    key_all = jnp.concatenate([far_pair[0], near_pair[0], key], 0).reshape(
        3 * tok_rows, kv_heads, HEAD_SIZE
    )
    value_all = jnp.concatenate([far_pair[1], near_pair[1], value], 0).reshape(
        3 * tok_rows, kv_heads, HEAD_SIZE
    )
    key_pos = positions[0] - 2 * tok_rows + jnp.arange(3 * tok_rows, dtype=jnp.int32)
    visible = (key_pos[None, :] >= lower[:, None]) & (key_pos[None, :] <= positions[:, None])
    grad_qry, grad_key, grad_val = attend(
        query_rows,
        key_all,
        value_all,
        visible,
        logsumexp_rows,
        output_grad_rows,
        row_delta,
        score_scale,
    )
    key_parts = grad_key.reshape(3, tok_rows, key_value_width)
    value_parts = grad_val.reshape(3, tok_rows, key_value_width)
    key_far, key_near, key_own = (key_parts[0], key_parts[1], key_parts[2])
    value_far, value_near, value_own = (value_parts[0], value_parts[1], value_parts[2])
    back_near = shifted((key_near, value_near), "seq", -1)
    back_far = shifted((key_far, value_far), "seq", -2)
    key_total = key_own + back_near[0] + back_far[0]
    value_total = value_own + back_near[1] + back_far[1]
    q_grad_low = grad_qry.reshape(tok_rows, q_heads * HEAD_SIZE).astype(jnp.bfloat16)
    k_grad_low = key_total.astype(jnp.bfloat16)
    v_grad_low = value_total.astype(jnp.bfloat16)
    partial_sum = projector(q_grad_low, lax.all_gather(w_query, "seq", axis=0, tiled=True))
    partial_sum = partial_sum + projector(
        k_grad_low, lax.all_gather(key_weight, "seq", axis=0, tiled=True)
    )
    partial_sum = partial_sum + projector(
        v_grad_low, lax.all_gather(value_weight, "seq", axis=0, tiled=True)
    )
    summed = lax.psum_scatter(partial_sum, "head", scatter_dimension=1, tiled=True)
    return summed.astype(jnp.bfloat16)


def solution(mesh):
    in_specs = (
        P("seq", "head"),
        P("seq", "head"),
        P("seq", "head"),
        P("seq", "head"),
        P("seq", "head"),
        P("head", "seq"),
        P(),
        P("seq", "head"),
        P("seq", "head"),
        P("seq", "head"),
    )
    out_specs = P("seq", "head")
    return jax.shard_map(shards, mesh=mesh, in_specs=in_specs, out_specs=out_specs, check_vma=False)
```

profile of v0, /device:TPU:1, one launch (start us, length us, event | category | flops | bytes accessed | tf_op | source)
XLA Modules:
  0.0 768.8 jit_solution(6138011124968313008)
XLA Ops:
  6.5 0.7 all-gather.9.cloned.1.call-update
  7.3 0.7 all-gather.11.cloned.1.call-update
  8.1 0.7 all-gather.7.cloned.1.call-update
  8.8 1.0 copy.61
  9.8 4.9 collective-permute-start.3
  14.7 3.5 collective-permute-start.2
  18.3 1.0 copy.54
  19.3 2.2 collective-permute-start.1
  21.5 3.5 collective-permute-start
  25.1 0.6 copy-done.1
  25.6 0.5 slice.27
  26.2 0.7 sub.31
  26.9 0.7 copy.57
  27.7 0.1 reduce.1
  27.8 1.2 sub.30
  29.0 1.5 copy.64
  30.5 1.5 copy.58
  32.0 1.5 copy.93
  34.1 0.8 select_reduce_fusion
  34.9 0.9 compare_and_fusion
  35.8 0.3 fusion.9
  36.1 1.6 fusion.21
  37.7 2.4 fusion.10
  40.2 0.1 fusion.19
  40.3 1.3 collective-permute-start.7
  41.6 2.4 collective-permute-start.6
  44.0 4.0 fusion.2
  48.0 1.9 convolution_bitcast_fusion
  49.9 0.1 fusion.20
  50.0 1.3 collective-permute-start.5
  51.3 2.1 collective-permute-start.4
  53.4 0.9 convolution_convert_fusion
  54.3 0.6 collective-permute-done.6
  55.0 7.5 collective-permute-done.5
  62.5 2.8 collective-permute-done.4
  65.3 0.1 fusion.16
  65.3 172.2 %all-gather.9.cloned.1.call-done = bf16[128,28,256]{2,1,0:T(8,128)(2,1)} async-done(((bf16[1,28,256]{2,1,0:T(8,128)(2,1)}), bf16[128,28,256]{2,1,0:T(8,128)(2,1)}) %all-gather.9.cloned.1.call-update) | async-done | bytes 1835024 | tf_op jit(solution)/shard_map/all_gather | solution.py:110
  237.5 2.5 reshape.141
  240.0 210.2 %all-gather.11.cloned.1.call-done = bf16[128,28,256]{2,1,0:T(8,128)(2,1)} async-done(((bf16[1,28,256]{2,1,0:T(8,128)(2,1)}), bf16[128,28,256]{2,1,0:T(8,128)(2,1)}) %all-gather.11.cloned.1.call-update) | async-done | bytes 1835024 | tf_op jit(solution)/shard_map/all_gather | solution.py:113
  450.1 3.8 reshape.143
  453.9 222.8 %all-gather.7.cloned.1.call-done = bf16[128,28,1792]{2,1,0:T(8,128)(2,1)} async-done(((bf16[1,28,1792]{2,1,0:T(8,128)(2,1)}), bf16[128,28,1792]{2,1,0:T(8,128)(2,1)}) %all-gather.7.cloned.1.call-update) | async-done | bytes 12845072 | tf_op jit(solution)/shard_map/all_gather | solution.py:108
  676.7 17.6 %reshape.139 = bf16[3584,1792]{1,0:T(8,128)(2,1)} reshape(bf16[128,28,1792]{2,1,0:T(8,128)(2,1)} %all-gather.7.cloned.1.call-done) | data formatting | bytes 25690112
  694.3 6.6 fusion.22
  701.0 0.7 convolution_add_fusion.1
  701.7 0.8 copy-done
  702.5 2.5 convolution_add_fusion
  705.0 54.7 %reduce-scatter.2.cloned.1.call-done = f32[256,1792]{1,0:T(8,128)} async-done(((f32[256,3584]{1,0:T(8,128)}), f32[256,1792]{1,0:T(8,128)}) %reduce-scatter.2.cloned.1.call-update) | async-done | bytes 1835024 | tf_op jit(solution)/shard_map/reduce_scatter | solution.py:115
  759.7 2.5 convert_element_type.31
  (19 shorter events, 0.3 us)
Async XLA Ops:
  6.5 231.0 %all-gather.9.cloned.1.call-start = ((), (), s32[]{:S(2)}) async-start(), calls=%async_computation.3 | async-start | bytes 2113536 | tf_op jit(solution)/shard_map/all_gather | solution.py:110
  7.3 442.9 %all-gather.11.cloned.1.call-start = ((), (), s32[]{:S(2)}) async-start(), calls=%async_computation.4 | async-start | bytes 2113536 | tf_op jit(solution)/shard_map/all_gather | solution.py:113
  8.0 668.7 %all-gather.7.cloned.1.call-start = ((), (), s32[]{:S(2)}) async-start(), calls=%async_computation.2 | async-start | bytes 14794752 | tf_op jit(solution)/shard_map/all_gather | solution.py:108
  8.7 751.0 %reduce-scatter.2.cloned.1.call-start = ((), (), s32[]{:S(2)}) async-start(), calls=%async_computation.1 | async-start | bytes 5505024 | tf_op jit(solution)/shard_map/reduce_scatter | solution.py:115
  9.8 34.2 %collective-permute-start.3 = (bf16[256,256]{0,1:T(8,128)(2,1)S(1)}, bf16[256,256]{0,1:T(8,128)(2,1)S(1)}, u32[]{:S(2)}, u32[]{:S(2)}) collective-permute-start(bf16[256,256]{0,1:T(8,128)(2,1)S(1)} %copy.61), channel_id=1, source_target_pairs={{0,2},{2,4},{4,6},{6,8},{8,10},{10,12},{12,14},{14,16},{16,18},{18... | collective-permute-start | bytes 393224 | tf_op jit(solution)/shard_map/ppermute | solution.py:14
  14.7 29.3 %collective-permute-start.2 = (bf16[256,256]{0,1:T(8,128)(2,1)S(1)}, bf16[256,256]{0,1:T(8,128)(2,1)S(1)}, u32[]{:S(2)}, u32[]{:S(2)}) collective-permute-start(bf16[256,256]{0,1:T(8,128)(2,1)S(1)} %copy.61), channel_id=1, source_target_pairs={{0,4},{2,6},{4,8},{6,10},{8,12},{10,14},{12,16},{14,18},{16,20},{1... | collective-permute-start | bytes 393224 | tf_op jit(solution)/shard_map/ppermute | solution.py:14
  19.3 16.8 %collective-permute-start.1 = (bf16[256,256]{0,1:T(8,128)(2,1)S(1)}, bf16[256,256]{0,1:T(8,128)(2,1)S(1)}, u32[]{:S(2)}, u32[]{:S(2)}) collective-permute-start(bf16[256,256]{0,1:T(8,128)(2,1)S(1)} %copy.54), channel_id=1, source_target_pairs={{0,2},{2,4},{4,6},{6,8},{8,10},{10,12},{12,14},{14,16},{16,18},{18... | collective-permute-start | bytes 393224 | tf_op jit(solution)/shard_map/ppermute | solution.py:14
  21.5 14.6 %collective-permute-start = (bf16[256,256]{0,1:T(8,128)(2,1)S(1)}, bf16[256,256]{0,1:T(8,128)(2,1)S(1)}, u32[]{:S(2)}, u32[]{:S(2)}) collective-permute-start(bf16[256,256]{0,1:T(8,128)(2,1)S(1)} %copy.54), channel_id=1, source_target_pairs={{0,4},{2,6},{4,8},{6,10},{8,12},{10,14},{12,16},{14,18},{16,20},{1... | collective-permute-start | bytes 393224 | tf_op jit(solution)/shard_map/ppermute | solution.py:14
  25.1 0.6 copy-start.1
  40.3 14.0 %collective-permute-start.7 = (f32[256,256]{0,1:T(8,128)S(1)}, f32[256,256]{0,1:T(8,128)S(1)}, u32[]{:S(2)}, u32[]{:S(2)}) collective-permute-start(f32[256,256]{0,1:T(8,128)S(1)} %bitcast.104), channel_id=1, source_target_pairs={{4,0},{6,2},{8,4},{10,6},{12,8},{14,10},{16,12},{18,14},{20,16},{2... | collective-permute-start | bytes 786440 | tf_op jit(solution)/shard_map/ppermute | solution.py:14
  41.6 13.4 %collective-permute-start.6 = (f32[256,256]{0,1:T(8,128)S(1)}, f32[256,256]{0,1:T(8,128)S(1)}, u32[]{:S(2)}, u32[]{:S(2)}) collective-permute-start(f32[256,256]{0,1:T(8,128)S(1)} %bitcast.103), channel_id=1, source_target_pairs={{2,0},{4,2},{6,4},{8,6},{10,8},{12,10},{14,12},{16,14},{18,16},{20... | collective-permute-start | bytes 786440 | tf_op jit(solution)/shard_map/ppermute | solution.py:14
  50.0 12.5 %collective-permute-start.5 = (f32[256,256]{0,1:T(8,128)S(1)}, f32[256,256]{0,1:T(8,128)S(1)}, u32[]{:S(2)}, u32[]{:S(2)}) collective-permute-start(f32[256,256]{0,1:T(8,128)S(1)} %bitcast.106), channel_id=1, source_target_pairs={{4,0},{6,2},{8,4},{10,6},{12,8},{14,10},{16,12},{18,14},{20,16},{2... | collective-permute-start | bytes 786440 | tf_op jit(solution)/shard_map/ppermute | solution.py:14
  51.3 14.0 %collective-permute-start.4 = (f32[256,256]{0,1:T(8,128)S(1)}, f32[256,256]{0,1:T(8,128)S(1)}, u32[]{:S(2)}, u32[]{:S(2)}) collective-permute-start(f32[256,256]{0,1:T(8,128)S(1)} %bitcast.105), channel_id=1, source_target_pairs={{2,0},{4,2},{6,4},{8,6},{10,8},{12,10},{14,12},{16,14},{18,16},{20... | collective-permute-start | bytes 786440 | tf_op jit(solution)/shard_map/ppermute | solution.py:14
  701.0 1.5 copy-start
Sparse Core Ops, SparseCore 0:
  9.2 228.2 all-gather.8
  239.4 210.7 all-gather.10
  452.0 224.6 all-gather.6
  705.1 54.5 reduce-scatter.1
where the time goes:
time: 770 us; the launch traced here: 769 us
  waiting for transfers between devices  673 us (87%)
  local copies, waits for them, and re-layouts  33.7 us (4%)
  starting transfers between devices  21.4 us (3%)
  matrix products  20.7 us (3%)
  between operations  14.1 us (2%)
    all_gather x1, waiting for transfers between devices, shards(): lax.all_gather(w_query, 'seq', axis=0, tiled=True)  223 us
    all_gather x1, waiting for transfers between devices, shards(): lax.all_gather(value_weight, 'seq', axis=0, tiled=True)  210 us
    all_gather x1, waiting for transfers between devices, shards(): lax.all_gather(key_weight, 'seq', axis=0, tiled=True)  172 us
    reduce_scatter x1, waiting for transfers between devices, shards(): lax.psum_scatter(partial_sum, 'head', scatter_dimension=1, tiled=True)  54.7 us
    unnamed x12, local copies, waits for them, and re-layouts  31.6 us
    ppermute x8, starting transfers between devices, shifted(): return lax.ppermute(array, axis, pairs)  21.3 us
  transfers between devices with their start and end apart: 12, of which 7 were waited for; matrix products, arithmetic and copies ran while one was open for 4% of the time, Pallas kernels for 0%

commit v1 on v0

--- a/solution.py
+++ b/solution.py
@@ -105,7 +105,12 @@
     q_grad_low = grad_qry.reshape(tok_rows, q_heads * HEAD_SIZE).astype(jnp.bfloat16)
     k_grad_low = key_total.astype(jnp.bfloat16)
     v_grad_low = value_total.astype(jnp.bfloat16)
-    partial_sum = projector(q_grad_low, lax.all_gather(w_query, "seq", axis=0, tiled=True))
+    partial_sum = projector(
+        q_grad_low,
+        jnp.concatenate(
+            lax.all_to_all(jnp.stack([w_query] * lax.axis_size("seq")), "seq", 0, 0), axis=0
+        ),
+    )
     partial_sum = partial_sum + projector(
         k_grad_low, lax.all_gather(key_weight, "seq", axis=0, tiled=True)
     )

time: 770 us -> 658 us (0.85)
  waiting for transfers between devices: 673 us -> 546 us
  starting transfers between devices: 21.4 us -> 34.2 us
    ppermute x8, waiting for transfers between devices: 10.9 us -> 325 us  [shifted(): return lax.ppermute(array, axis, pairs)]
    all_gather x1 -> x0, waiting for transfers between devices: 223 us -> none  [shards(): lax.all_gather(w_query, 'seq', axis=0, tiled=True)]
    all_gather x1, waiting for transfers between devices: 172 us -> 0.02 us  [shards(): lax.all_gather(key_weight, 'seq', axis=0, tiled=True)]
    all_gather x1, waiting for transfers between devices: 210 us -> 166 us  [shards(): lax.all_gather(value_weight, 'seq', axis=0, tiled=True)]
    unnamed x12 -> x23, local copies, waits for them, and re-layouts: 31.6 us -> 9.75 us
    reshape x0 -> x1, local copies, waits for them, and re-layouts: none -> 17.7 us  [shards(): jnp.concatenate(lax.all_to_all(jnp.stack([w_query] * lax.axis_size('seq')...]
    all_to_all x0 -> x1, starting transfers between devices: none -> 15.4 us  [shards(): lax.all_to_all(jnp.stack([w_query] * lax.axis_size('seq')), 'seq', 0, 0)]
  transfers between devices with their start and end apart: 12 -> 12, of which waited for: 7 -> 6; matrix products, arithmetic and copies ran while one was open for 4% -> 4% of each run, Pallas kernels for 0% -> 0%
where the time goes in v1:
time: 658 us; the launch traced here: 657 us
  waiting for transfers between devices  546 us (83%)
  local copies, waits for them, and re-layouts  36.1 us (5%)
  starting transfers between devices  34.2 us (5%)
  matrix products  20.7 us (3%)
  between operations  14.1 us (2%)
    ppermute x8, waiting for transfers between devices, shifted(): return lax.ppermute(array, axis, pairs)  325 us
    all_gather x1, waiting for transfers between devices, shards(): lax.all_gather(value_weight, 'seq', axis=0, tiled=True)  166 us
    reduce_scatter x1, waiting for transfers between devices, shards(): lax.psum_scatter(partial_sum, 'head', scatter_dimension=1, tiled=True)  54.3 us
    ppermute x8, starting transfers between devices, shifted(): return lax.ppermute(array, axis, pairs)  18.6 us
    reshape x1, local copies, waits for them, and re-layouts, shards(): jnp.concatenate(lax.all_to_all(jnp.stack([w_query] * lax.axis_size('seq')...  17.7 us
    all_to_all x1, starting transfers between devices, shards(): lax.all_to_all(jnp.stack([w_query] * lax.axis_size('seq')), 'seq', 0, 0)  15.4 us
  transfers between devices with their start and end apart: 12, of which 6 were waited for; matrix products, arithmetic and copies ran while one was open for 4% of the time, Pallas kernels for 0%

profile of v1, /device:TPU:1, one launch (start us, length us, event | category | flops | bytes accessed | tf_op | source)
XLA Modules:
  0.0 656.6 jit_solution(16018776410200825300)
XLA Ops:
  6.5 7.9 %stack.2 = bf16[128,28,1792]{2,1,0:T(8,128)(2,1)} broadcast(bf16[28,1792]{1,0:T(8,128)(2,1)} %param.17), dimensions={1,2} | broadcast | bytes 12945408 | tf_op jit(solution)/shard_map/stack | solution.py:111
  14.5 15.4 %all-to-all-start = ((bf16[128,28,1792]{2,1,0:T(8,128)(2,1)}), bf16[128,28,1792]{2,1,0:T(8,128)(2,1)}, u32[]{:S(2)}, u32[]{:S(2)}) async-start(bf16[128,28,1792]{2,1,0:T(8,128)(2,1)} %stack.2), calls=%async_computation | async-start | bytes 29360128 | tf_op jit(solution)/shard_map/all_to_all | solution.py:111
  29.9 0.7 all-gather.5.cloned.1.call-update
  30.7 0.1 copy.61
  30.8 3.5 collective-permute-start.3
  34.3 3.1 collective-permute-start.2
  37.4 0.1 copy.54
  37.5 2.3 collective-permute-start.1
  39.8 3.1 collective-permute-start
  43.0 0.0 reduce-scatter.2.cloned.1.call-start
  43.1 0.6 slice.27
  43.7 0.1 copy.57
  43.7 0.1 reduce-window.9
  43.8 0.1 reduce.1
  43.9 0.5 sub.30
  44.4 0.5 copy.64
  45.0 0.5 copy.58
  45.5 1.5 copy.93
  47.6 0.8 select_reduce_fusion
  48.4 0.9 compare_and_fusion
  49.3 0.3 fusion.9
  49.6 314.0 %collective-permute-done.1 = bf16[256,256]{0,1:T(8,128)(2,1)S(1)} collective-permute-done((bf16[256,256]{0,1:T(8,128)(2,1)S(1)}, bf16[256,256]{0,1:T(8,128)(2,1)S(1)}, u32[]{:S(2)}, u32[]{:S(2)}) %collective-permute-start.1) | collective-permute-done | bytes 131104 | tf_op jit(solution)/shard_map/ppermute | solution.py:14
  363.6 1.4 collective-permute-done
  365.0 1.6 fusion.21
  366.7 2.4 fusion.10
  369.1 0.1 fusion.19
  369.2 1.3 collective-permute-start.7
  370.5 1.9 collective-permute-start.6
  372.5 4.0 fusion.2
  376.5 1.9 convolution_bitcast_fusion
  378.4 0.1 fusion.20
  378.4 1.3 collective-permute-start.5
  379.7 2.1 collective-permute-start.4
  381.8 0.9 convolution_convert_fusion
  382.8 0.1 fusion.14
  382.8 8.7 %collective-permute-done.5 = f32[256,256]{0,1:T(8,128)S(1)} collective-permute-done((f32[256,256]{0,1:T(8,128)S(1)}, f32[256,256]{0,1:T(8,128)S(1)}, u32[]{:S(2)}, u32[]{:S(2)}) %collective-permute-start.5) | collective-permute-done | bytes 262176 | tf_op jit(solution)/shard_map/ppermute | solution.py:14
  391.5 1.0 collective-permute-done.4
  392.5 0.1 fusion.16
  392.6 2.5 reshape.145
  395.1 166.0 %all-gather.7.cloned.1.call-done = bf16[128,28,256]{2,1,0:T(8,128)(2,1)} async-done(((bf16[1,28,256]{2,1,0:T(8,128)(2,1)}), bf16[128,28,256]{2,1,0:T(8,128)(2,1)}) %all-gather.7.cloned.1.call-update) | async-done | bytes 1835024 | tf_op jit(solution)/shard_map/all_gather | solution.py:118
  561.1 3.8 reshape.147
  564.9 17.7 %reshape.143 = bf16[3584,1792]{1,0:T(8,128)(2,1)} reshape(bf16[128,28,1792]{2,1,0:T(8,128)(2,1)} %all-to-all-done) | data formatting | bytes 25690112 | tf_op jit(solution)/shard_map/reshape | solution.py:110
  582.5 6.6 %fusion.22 = f32[256,3584]{1,0:T(8,128)S(1)} fusion(bf16[256,1792]{0,1:T(8,128)(2,1)S(1)} %bitcast.100, bf16[3584,1792]{1,0:T(8,128)(2,1)} %reshape.143), kind=kOutput, calls=%fused_computation.35 | convolution fusion | flops 3288334336 | bytes 17432576 | tf_op jit(solution)/shard_map/tc,rc->tr/dot_general | solution.py:55
  589.2 0.7 convolution_add_fusion.1
  589.9 0.8 copy-done
  590.7 2.5 convolution_add_fusion
  593.2 54.3 %reduce-scatter.2.cloned.1.call-done = f32[256,1792]{1,0:T(8,128)} async-done(((f32[256,3584]{1,0:T(8,128)}), f32[256,1792]{1,0:T(8,128)}) %reduce-scatter.2.cloned.1.call-update) | async-done | bytes 1835024 | tf_op jit(solution)/shard_map/reduce_scatter | solution.py:120
  647.6 2.5 convert_element_type.31
  (31 shorter events, 0.3 us)
Async XLA Ops:
  14.4 16.2 %copy-start.3 = (bf16[256,256]{1,0:T(8,128)(2,1)S(1)}, bf16[256,256]{1,0:T(8,128)(2,1)}, u32[]{:S(2)}) copy-start(bf16[256,256]{1,0:T(8,128)(2,1)} %param.12) | copy-start | bytes 393220
  14.4 23.0 %copy-start.4 = (bf16[256,256]{1,0:T(8,128)(2,1)S(1)}, bf16[256,256]{1,0:T(8,128)(2,1)}, u32[]{:S(2)}) copy-start(bf16[256,256]{1,0:T(8,128)(2,1)} %param.11) | copy-start | bytes 393220
  14.4 29.2 %copy-start.5 = (f32[14,256]{1,0:T(8,128)S(1)}, f32[14,256]{1,0:T(8,128)}, u32[]{:S(2)}) copy-start(f32[14,256]{1,0:T(8,128)} %param.15) | copy-start | bytes 43012
  14.4 29.2 %copy-start.7 = (s32[32]{0:T(128)S(1)}, s32[32]{0:T(128)}, u32[]{:S(2)}) copy-start(s32[32]{0:T(128)} %param.16) | copy-start | bytes 388
  14.4 30.0 %copy-start.1 = (bf16[256,1792]{1,0:T(8,128)(2,1)S(1)}, bf16[256,1792]{1,0:T(8,128)(2,1)}, u32[]{:S(2)}) copy-start(bf16[256,1792]{1,0:T(8,128)(2,1)} %param.14) | copy-start | bytes 2752516
  14.5 30.5 %copy-start.2 = (bf16[256,1792]{1,0:T(8,128)(2,1)S(1)}, bf16[256,1792]{1,0:T(8,128)(2,1)}, u32[]{:S(2)}) copy-start(bf16[256,1792]{1,0:T(8,128)(2,1)} %param.10) | copy-start | bytes 2752516
  14.5 550.4 %all-to-all-start = ((bf16[128,28,1792]{2,1,0:T(8,128)(2,1)}), bf16[128,28,1792]{2,1,0:T(8,128)(2,1)}, u32[]{:S(2)}, u32[]{:S(2)}) async-start(bf16[128,28,1792]{2,1,0:T(8,128)(2,1)} %stack.2), calls=%async_computation | async-start | bytes 29360128 | tf_op jit(solution)/shard_map/all_to_all | solution.py:111
  29.9 362.8 %all-gather.5.cloned.1.call-start = ((), (), s32[]{:S(2)}) async-start(), calls=%async_computation.3 | async-start | bytes 2113536 | tf_op jit(solution)/shard_map/all_gather | solution.py:115
  30.6 530.5 %all-gather.7.cloned.1.call-start = ((), (), s32[]{:S(2)}) async-start(), calls=%async_computation.4 | async-start | bytes 2113536 | tf_op jit(solution)/shard_map/all_gather | solution.py:118
  30.8 341.7 %collective-permute-start.3 = (bf16[256,256]{0,1:T(8,128)(2,1)S(1)}, bf16[256,256]{0,1:T(8,128)(2,1)S(1)}, u32[]{:S(2)}, u32[]{:S(2)}) collective-permute-start(bf16[256,256]{0,1:T(8,128)(2,1)S(1)} %copy.61), channel_id=1, source_target_pairs={{0,2},{2,4},{4,6},{6,8},{8,10},{10,12},{12,14},{14,16},{16,18},{18... | collective-permute-start | bytes 393224 | tf_op jit(solution)/shard_map/ppermute | solution.py:14
  34.3 338.1 %collective-permute-start.2 = (bf16[256,256]{0,1:T(8,128)(2,1)S(1)}, bf16[256,256]{0,1:T(8,128)(2,1)S(1)}, u32[]{:S(2)}, u32[]{:S(2)}) collective-permute-start(bf16[256,256]{0,1:T(8,128)(2,1)S(1)} %copy.61), channel_id=1, source_target_pairs={{0,4},{2,6},{4,8},{6,10},{8,12},{10,14},{12,16},{14,18},{16,20},{1... | collective-permute-start | bytes 393224 | tf_op jit(solution)/shard_map/ppermute | solution.py:14
  37.5 326.1 %collective-permute-start.1 = (bf16[256,256]{0,1:T(8,128)(2,1)S(1)}, bf16[256,256]{0,1:T(8,128)(2,1)S(1)}, u32[]{:S(2)}, u32[]{:S(2)}) collective-permute-start(bf16[256,256]{0,1:T(8,128)(2,1)S(1)} %copy.54), channel_id=1, source_target_pairs={{0,2},{2,4},{4,6},{6,8},{8,10},{10,12},{12,14},{14,16},{16,18},{18... | collective-permute-start | bytes 393224 | tf_op jit(solution)/shard_map/ppermute | solution.py:14
  39.8 325.2 %collective-permute-start = (bf16[256,256]{0,1:T(8,128)(2,1)S(1)}, bf16[256,256]{0,1:T(8,128)(2,1)S(1)}, u32[]{:S(2)}, u32[]{:S(2)}) collective-permute-start(bf16[256,256]{0,1:T(8,128)(2,1)S(1)} %copy.54), channel_id=1, source_target_pairs={{0,4},{2,6},{4,8},{6,10},{8,12},{10,14},{12,16},{14,18},{16,20},{1... | collective-permute-start | bytes 393224 | tf_op jit(solution)/shard_map/ppermute | solution.py:14
  43.0 604.6 %reduce-scatter.2.cloned.1.call-start = ((), (), s32[]{:S(2)}) async-start(), calls=%async_computation.2 | async-start | bytes 5505024 | tf_op jit(solution)/shard_map/reduce_scatter | solution.py:120
  43.0 0.6 copy-start.6
  369.2 13.6 %collective-permute-start.7 = (f32[256,256]{0,1:T(8,128)S(1)}, f32[256,256]{0,1:T(8,128)S(1)}, u32[]{:S(2)}, u32[]{:S(2)}) collective-permute-start(f32[256,256]{0,1:T(8,128)S(1)} %bitcast.103), channel_id=1, source_target_pairs={{4,0},{6,2},{8,4},{10,6},{12,8},{14,10},{16,12},{18,14},{20,16},{2... | collective-permute-start | bytes 786440 | tf_op jit(solution)/shard_map/ppermute | solution.py:14
  370.5 12.3 %collective-permute-start.6 = (f32[256,256]{0,1:T(8,128)S(1)}, f32[256,256]{0,1:T(8,128)S(1)}, u32[]{:S(2)}, u32[]{:S(2)}) collective-permute-start(f32[256,256]{0,1:T(8,128)S(1)} %bitcast.102), channel_id=1, source_target_pairs={{2,0},{4,2},{6,4},{8,6},{10,8},{12,10},{14,12},{16,14},{18,16},{20... | collective-permute-start | bytes 786440 | tf_op jit(solution)/shard_map/ppermute | solution.py:14
  378.4 13.1 %collective-permute-start.5 = (f32[256,256]{0,1:T(8,128)S(1)}, f32[256,256]{0,1:T(8,128)S(1)}, u32[]{:S(2)}, u32[]{:S(2)}) collective-permute-start(f32[256,256]{0,1:T(8,128)S(1)} %bitcast.105), channel_id=1, source_target_pairs={{4,0},{6,2},{8,4},{10,6},{12,8},{14,10},{16,12},{18,14},{20,16},{2... | collective-permute-start | bytes 786440 | tf_op jit(solution)/shard_map/ppermute | solution.py:14
  379.7 12.8 %collective-permute-start.4 = (f32[256,256]{0,1:T(8,128)S(1)}, f32[256,256]{0,1:T(8,128)S(1)}, u32[]{:S(2)}, u32[]{:S(2)}) collective-permute-start(f32[256,256]{0,1:T(8,128)S(1)} %bitcast.104), channel_id=1, source_target_pairs={{2,0},{4,2},{6,4},{8,6},{10,8},{12,10},{14,12},{16,14},{18,16},{20... | collective-permute-start | bytes 786440 | tf_op jit(solution)/shard_map/ppermute | solution.py:14
  589.2 1.5 copy-start
Sparse Core Ops, SparseCore 0:
  32.6 276.9 all-gather.4
  311.5 249.6 all-gather.6
  593.4 54.1 reduce-scatter.1
